TPU v7x, 256 devices: a whole 4x4x8 slice. The times are simulated.
256 devices in a mesh: section: 2 (over z_lo), owner: 32 (over x, z_hi, core), context: 4 (over y).
Axes of the slice: x: 4, y: 4, z: 8 (z_hi: 4, z_lo: 2; z = z_hi * 2 + z_lo), core: 2. Of those that a mesh axis runs over, the one named last changes fastest.
Arguments:
- x_attn: bfloat16 [16384, 8192], P(('section', 'context'), 'owner'), parts along dimension 0, may hold values from -6 to 6
- x_mlp: bfloat16 [16384, 8192], P(('section', 'context'), 'owner'), parts along dimension 0, may hold values from -6 to 6
- x_down: bfloat16 [16384, 29568], P(('section', 'context'), 'owner'), parts along dimension 0, may hold values from -6 to 6
- omega_attn: bfloat16 [16384, 256], P(('section', 'owner')), parts along dimension 0, may hold values from -6 to 6
- omega_mlp: bfloat16 [16384, 256], P(('section', 'owner')), parts along dimension 0, may hold values from -6 to 6
- omega_down: bfloat16 [59136, 256], P(('section', 'owner')), parts along dimension 0, may hold values from -6 to 6
- basis_attn: bfloat16 [16384, 256], P(('section', 'owner')), parts along dimension 0, may hold values from -1 to 1
- basis_mlp: bfloat16 [16384, 256], P(('section', 'owner')), parts along dimension 0, may hold values from -1 to 1
- basis_down: bfloat16 [59136, 256], P(('section', 'owner')), parts along dimension 0, may hold values from -1 to 1
- eig_attn: float32 [512], P('section'), parts along dimension 0, may hold values from 2 to 20
- eig_mlp: float32 [512], P('section'), parts along dimension 0, may hold values from 2 to 20
- eig_down: float32 [512], P('section'), parts along dimension 0, may hold values from 2 to 20
Outputs:
- sketch_attn: float32 [16384, 256], P(('section', 'owner', 'context')), parts along dimension 0
- sketch_mlp: float32 [16384, 256], P(('section', 'owner', 'context')), parts along dimension 0
- sketch_down: float32 [59136, 256], P(('section', 'owner', 'context')), parts along dimension 0
There are 2 independent parts, one for each index of `section`. A program takes and returns all parts, laid end to end along the dimension named above; each array names one. Nothing has to cross between parts.
All inputs are finite; a program needn't handle non-finite values.
Results may differ from a plain program's by a relative error of at most 0.0003.
Values may be sent and summed in bfloat16 or wider, within the bound.
A program may use at most 64 MiB of HBM per device.

v0:
```python
import jax
import jax.numpy as jnp
from jax import lax
from jax.sharding import PartitionSpec as P


def token_contract(inputs, probe):
    return lax.dot_general(
        inputs, probe, (((0,), (0,)), ((), ())), preferred_element_type=jnp.float32
    )


def prior_rows(basis, eigen, core):
    rows = basis.shape[0] // lax.axis_size("context")
    picked = lax.dynamic_slice_in_dim(basis, lax.axis_index("context") * rows, rows, 0)
    weighted = eigen[:, None] * core
    return 0.9 * jnp.dot(picked.astype(jnp.float32), weighted, precision=lax.Precision.HIGHEST)


def factor_share(inputs, probe):
    return lax.psum_scatter(
        token_contract(inputs, probe), "context", scatter_dimension=0, tiled=True
    )


def per_device(
    x_attn,
    x_mlp,
    x_down,
    omega_attn,
    omega_mlp,
    omega_down,
    basis_attn,
    basis_mlp,
    basis_down,
    eig_attn,
    eig_mlp,
    eig_down,
):
    inputs = (x_attn, x_mlp, x_down)
    omegas = (omega_attn, omega_mlp, omega_down)
    bases = (basis_attn, basis_mlp, basis_down)
    eigens = (eig_attn, eig_mlp, eig_down)
    total = x_attn.shape[0] * lax.axis_size("context")
    probes_local = [
        jnp.dot(x, w, preferred_element_type=jnp.float32) for x, w in zip(inputs, omegas)
    ]
    cores_local = [token_contract(b, w) for b, w in zip(bases, omegas)]
    summed = lax.psum(
        (
            probes_local[0],
            probes_local[1],
            probes_local[2],
            cores_local[0],
            cores_local[1],
            cores_local[2],
        ),
        "owner",
    )
    cores = summed[3:]
    datas = [factor_share(x, z.astype(jnp.bfloat16)) for x, z in zip(inputs, summed[:3])]
    results = [
        prior_rows(b, e, c) + 0.1 / total * d for b, e, c, d in zip(bases, eigens, cores, datas)
    ]
    return (results[0], results[1], results[2])


def solution(mesh):
    placed = (
        P(("section", "context"), "owner"),
        P(("section", "context"), "owner"),
        P(("section", "context"), "owner"),
        P(("section", "owner"), None),
        P(("section", "owner"), None),
        P(("section", "owner"), None),
        P(("section", "owner"), None),
        P(("section", "owner"), None),
        P(("section", "owner"), None),
        P("section"),
        P("section"),
        P("section"),
    )
    return jax.shard_map(
        per_device,
        mesh=mesh,
        in_specs=placed,
        out_specs=(
            P(("section", "owner", "context"), None),
            P(("section", "owner", "context"), None),
            P(("section", "owner", "context"), None),
        ),
        check_vma=False,
    )
```

profile of v0, /device:TPU:1, one launch (start us, length us, event | category | flops | bytes accessed | tf_op | source)
XLA Modules:
  0.0 527.0 jit_solution(6762687562577989676)
XLA Ops:
  8.0 0.0 copy-start
  8.0 0.0 reduce-scatter.7.cloned.1.call-start
  8.1 0.0 copy-start.9
  8.1 0.0 copy-start.11
  8.1 1.8 fusion.22
  9.9 0.0 copy-done
  9.9 2.7 fusion.24
  12.6 0.0 copy-done.9
  12.6 0.0 copy-done.11
  12.6 2.7 fusion.26
  15.3 0.0 copy-start.3
  15.3 0.0 copy-start.4
  15.3 199.1 %all-reduce.8 = (bf16[2048,256]{1,0:T(8,128)(2,1)}, bf16[2048,256]{1,0:T(8,128)(2,1)}, bf16[2048,256]{1,0:T(8,128)(2,1)}) all-reduce(f32[2048,256]{1,0:T(8,128)S(1)} %fusion.22, f32[2048,256]{1,0:T(8,128)} %fusion.24, f32[2048,256]{1,0:T(8,128)} %fusion.26), channel_id=1, replica_groups=mesh['section'=2,'owner'=32,'context'=4] {'owner'}, use_global_device_ids=true, to_apply=%region_1.0 | all-reduce | flops 1572864 | bytes 9437184 | tf_op jit(solution)/shard_map/psum | solution.py:49
  214.4 0.0 copy-start.10
  214.4 2.6 convolution_bitcast_fusion.1
  217.0 0.0 reduce-scatter.7.cloned.1.call-update
  217.1 0.0 all-reduce.7.cloned.1.call-start
  217.1 0.0 copy-done.2
  217.1 1.8 fusion.21
  219.0 0.0 copy-done.3
  219.0 0.0 copy-done.4
  219.0 0.9 fusion.23
  219.9 2.2 fusion.25
  222.1 0.0 all-reduce.7.cloned.1.call-update
  222.1 0.0 reduce-scatter.5.cloned.1.call-start
  222.2 0.0 copy-done.1
  222.2 0.0 copy-done.10
  222.2 1.2 convolution_bitcast_fusion.2
  223.5 0.0 reduce-scatter.5.cloned.1.call-update
  223.5 0.0 copy-start.8
  223.5 0.0 copy-start.5
  223.5 0.0 copy-start.6
  223.5 0.0 copy-start.7
  223.5 3.6 convolution_bitcast_fusion
  227.1 15.7 %fusion = f32[232,256]{1,0:T(8,128)S(1)} fusion(f32[924,256]{1,0:T(8,128)S(1)} %convolution_bitcast_fusion), kind=kCustom, calls=%all-reduce-scatter | all-reduce-scatter fusion | flops 237569 | bytes 1184768
  242.8 4.0 collective-permute-start
  246.9 0.0 copy-done.8
  246.9 0.6 dynamic-slice.4
  248.1 0.0 collective-permute-done
  248.1 0.3 concatenate
  248.4 0.0 reduce-scatter.7.cloned.1.call-done
  248.5 265.3 %all-reduce.7.cloned.1.call-done = (f32[256,256]{1,0:T(8,128)}, f32[256,256]{1,0:T(8,128)}, f32[256,256]{1,0:T(8,128)}) async-done(((f32[256,256]{1,0:T(8,128)}, f32[256,256]{1,0:T(8,128)}, f32[256,256]{1,0:T(8,128)}), (f32[256,256]{1,0:T(8,128)}, f32[256,256]{1,0:T(8,128)}, f32[256,256]{1,0:T(8,128)})) %all-reduce.7.cloned.1.call-update) | async-done | bytes 786448 | tf_op jit(solution)/shard_map/psum | solution.py:49
  513.7 0.0 copy-done.5
  513.7 1.9 fusion.2
  515.6 0.0 copy-done.6
  515.6 2.1 fusion.9
  517.7 0.0 copy-done.7
  517.7 1.9 fusion.1
  (4 shorter events, 0.0 us)
Async XLA Ops:
  8.0 1.9 copy-start
  8.0 240.4 %reduce-scatter.7.cloned.1.call-start = ((), (), s32[]{:S(2)}) async-start(), calls=%async_computation.3 | async-start | bytes 327680 | tf_op jit(solution)/shard_map/reduce_scatter | solution.py:21
  8.1 4.6 copy-start.9
  8.1 4.6 copy-start.11
  15.3 201.8 %copy-start.2 = (bf16[256,256]{1,0:T(8,128)(2,1)S(1)}, bf16[256,256]{1,0:T(8,128)(2,1)}, u32[]{:S(2)}) copy-start(bf16[256,256]{1,0:T(8,128)(2,1)} %param.15) | copy-start | bytes 393220
  15.3 203.6 %copy-start.3 = (bf16[256,256]{1,0:T(8,128)(2,1)S(1)}, bf16[256,256]{1,0:T(8,128)(2,1)}, u32[]{:S(2)}) copy-start(bf16[256,256]{1,0:T(8,128)(2,1)} %param.16) | copy-start | bytes 393220
  15.3 203.6 %copy-start.4 = (bf16[256,256]{1,0:T(8,128)(2,1)S(1)}, bf16[256,256]{1,0:T(8,128)(2,1)}, u32[]{:S(2)}) copy-start(bf16[256,256]{1,0:T(8,128)(2,1)} %param.19) | copy-start | bytes 393220
  214.4 7.8 %copy-start.1 = (bf16[2048,256]{1,0:T(8,128)(2,1)S(1)}, bf16[2048,256]{1,0:T(8,128)(2,1)}, u32[]{:S(2)}) copy-start(bf16[2048,256]{1,0:T(8,128)(2,1)} %param.12) | copy-start | bytes 3145732
  214.4 7.8 %copy-start.10 = (bf16[2048,256]{1,0:T(8,128)(2,1)S(1)}, bf16[2048,256]{1,0:T(8,128)(2,1)}, u32[]{:S(2)}) copy-start(bf16[2048,256]{1,0:T(8,128)(2,1)} %get-tuple-element.3) | copy-start | bytes 3145732
  217.1 296.7 %all-reduce.7.cloned.1.call-start = ((), (), s32[]{:S(2)}) async-start(), calls=%async_computation.4 | async-start | bytes 1572864 | tf_op jit(solution)/shard_map/psum | solution.py:49
  222.1 295.5 %reduce-scatter.5.cloned.1.call-start = ((), (), s32[]{:S(2)}) async-start(), calls=%async_computation.2 | async-start | bytes 327680 | tf_op jit(solution)/shard_map/reduce_scatter | solution.py:21
  223.5 23.4 %copy-start.8 = (u32[256]{0:T(256)S(1)}, u32[256]{0:T(256)}, u32[]{:S(2)}) copy-start(u32[256]{0:T(256)} %constant.25) | copy-start | bytes 3076
  223.5 290.2 %copy-start.5 = (f32[256]{0:T(256)S(1)}, f32[256]{0:T(256)}, u32[]{:S(2)}) copy-start(f32[256]{0:T(256)} %param.22) | copy-start | bytes 3076
  223.5 292.1 %copy-start.6 = (f32[256]{0:T(256)S(1)}, f32[256]{0:T(256)}, u32[]{:S(2)}) copy-start(f32[256]{0:T(256)} %param.23) | copy-start | bytes 3076
  223.5 294.2 %copy-start.7 = (f32[256]{0:T(256)S(1)}, f32[256]{0:T(256)}, u32[]{:S(2)}) copy-start(f32[256]{0:T(256)} %param.21) | copy-start | bytes 3076
  242.8 5.3 %collective-permute-start = (f32[3,256]{1,0:T(4,128)S(1)}, f32[3,256]{1,0:T(4,128)S(1)}, u32[]{:S(2)}, u32[]{:S(2)}) collective-permute-start(f32[3,256]{1,0:T(4,128)S(1)} %slice), channel_id=1, source_target_pairs={{0,1},{1,2},{2,3},{4,5},{5,6},{6,7},{8,9},{9,10},{10,11},{12,13},{... | collective-permute-start | bytes 9224
Sparse Core Ops, SparseCore 0:
  217.2 25.3 reduce-scatter.6
  245.1 23.4 reduce-scatter.4
Sparse Core Ops, SparseCore 1:
  222.2 291.4 all-reduce.6
where the time goes:
time: 527 us
  waiting for transfers between devices  265 us (50%)
  blocking collectives  215 us (41%)
  matrix products  25.5 us (5%)
  between operations  16.3 us (3%)
    psum x1, waiting for transfers between devices, per_device(): lax.psum((probes_local[0], probes_local[1], probes_local[2], cores_local[...  265 us
    psum x1, blocking collectives, per_device(): lax.psum((probes_local[0], probes_local[1], probes_local[2], cores_local[...  199 us
    unnamed x1, blocking collectives  15.7 us
    dot_general x6, matrix products, token_contract(): lax.dot_general(inputs, probe, (((0,), (0,)), ((), ())), preferred_elemen...  12.4 us
  transfers between devices with their start and end apart: 4, of which 1 were waited for; matrix products, arithmetic and copies ran while one was open for 6% of the time, Pallas kernels for 0%

commit v1 on v0

v1 whole, which is shorter than its diff:
```python
import jax
import jax.numpy as jnp
from jax import lax
from jax.experimental import pallas as pl
from jax.experimental.pallas import tpu as pltpu
from jax.sharding import PartitionSpec as P

ORDER = (2, 0, 1)
SEMS = 40


def halves(rows, unit):
    a = -(-(rows // 2) // unit) * unit
    return a, rows - a


def sketch_kernel(total, tokens, turned, *refs):
    xs, ws, bs, es, outs = refs[0:3], refs[3:6], refs[6:9], refs[9:12], refs[12:15]
    s = refs[15]
    ssem, rsem, lsem = s["ssem"], s["rsem"], s["lsem"]
    owner, ctx = lax.axis_index("owner"), lax.axis_index("context")
    core, zi, xi = lax.rem(owner, 2), lax.rem(lax.div(owner, 2), 4), lax.div(owner, 8)

    def at(x, z, c):
        return {"owner": (lax.rem(x, 4) * 4 + lax.rem(z, 4)) * 2 + c}

    partner = at(xi, zi, 1 - core)
    xp, xm = at(xi + 1, zi, core), at(xi + 3, zi, core)
    zp, zm = at(xi, zi + 1, core), at(xi, zi + 3, core)
    yp, ym = {"context": lax.rem(ctx + 1, 4)}, {"context": lax.rem(ctx + 3, 4)}

    pending = []

    def remote(i, src, dst, dev):
        return pltpu.make_async_remote_copy(
            src_ref=src, dst_ref=dst, send_sem=ssem.at[i], recv_sem=rsem.at[i],
            device_id=dev, device_id_type=pl.DeviceIdType.MESH,
        )

    def send(i, src, dst, dev):
        copy = remote(i, src, dst, dev)
        copy.start()
        pending.append(copy)

    def recv(i, dst, dev):
        remote(i, dst, dst, dev).wait_recv()

    half = tokens // 2
    xv, wv, bv, ev = s["xv"], s["wv"], s["bv"], s["ev"]
    loads = {}
    for f in ORDER:
        loads["w", f] = pltpu.make_async_copy(ws[f], wv[f], lsem.at[f])
        for q, c in enumerate((1 - core, core)):
            rows = pl.ds(pl.multiple_of(c * half, half), half)
            where = (slice(None), rows) if turned[f] else rows
            loads["x", f, q] = pltpu.make_async_copy(
                xs[f].at[where], xv[f].at[where], lsem.at[3 + 2 * f + q])
        loads["b", f] = pltpu.make_async_copy(bs[f], bv[f], lsem.at[9 + f])
        loads["e", f] = pltpu.make_async_copy(es[f], ev[f], lsem.at[12 + f])
    for f in ORDER:
        for part in (("w", f), ("x", f, 0), ("x", f, 1)):
            loads[part].start()
    for f in ORDER:
        for part in (("b", f), ("e", f)):
            loads[part].start()

    barrier = pltpu.get_barrier_semaphore()
    for dev in (partner, xp, xm, zp, zm, yp, ym):
        pl.semaphore_signal(barrier, inc=1, device_id=dev, device_id_type=pl.DeviceIdType.MESH)
    pl.semaphore_wait(barrier, 7)

    def around(i):
        return lax.rem(i + 2, 4), lax.rem(i + 1, 4), lax.rem(i + 3, 4), i

    def rs_start(blocks, r1, r2, a, b, idx, devs, sem, pre):
        i2, ip, im, me = around(idx)
        plus, minus = devs
        pre(i2, 0)
        send(sem, blocks.at[i2, 0:a], r1.at[0, 0:a], plus)
        if b:
            send(sem + 1, blocks.at[i2, a:a + b], r1.at[1, 0:b], minus)
        pre(ip, 1)
        if b:
            send(sem + 2, blocks.at[ip, a:a + b], r2.at[0, a:a + b], plus)
        pre(im, 2)
        send(sem + 3, blocks.at[im, 0:a], r2.at[1, 0:a], minus)
        pre(me, 3)

    def rs_mid(blocks, r1, r2, a, b, idx, devs, sem):
        i2, ip, im, me = around(idx)
        plus, minus = devs
        recv(sem, r1.at[0, 0:a], plus)
        blocks[ip, 0:a] = blocks[ip, 0:a] + r1[0, 0:a]
        send(sem + 4, blocks.at[ip, 0:a], r2.at[0, 0:a], plus)
        if b:
            recv(sem + 1, r1.at[1, 0:b], minus)
            blocks[im, a:a + b] = blocks[im, a:a + b] + r1[1, 0:b]
            send(sem + 5, blocks.at[im, a:a + b], r2.at[1, a:a + b], minus)

    def rs_end(r2, a, b, devs, sem):
        plus, minus = devs
        recv(sem + 3, r2.at[1, 0:a], minus)
        recv(sem + 4, r2.at[0, 0:a], plus)
        if b:
            recv(sem + 2, r2.at[0, a:a + b], plus)
            recv(sem + 5, r2.at[1, a:a + b], minus)

    def ag_start(block, idx, devs, sem):
        for q, dev in enumerate(devs):
            send(sem + q, block(idx), block(idx), dev)

    def ag_mid(block, part, two, idx, devs, sem, got=None):
        i2, ip, im, me = around(idx)
        plus, minus = devs
        recv(sem, block(im), plus)
        send(sem + 2, part(im, 0), part(im, 0), plus)
        if got:
            got(im, 1)
        recv(sem + 1, block(ip), minus)
        if two:
            send(sem + 3, part(ip, 1), part(ip, 1), minus)
        if got:
            got(ip, 2)

    def ag_end(part, two, idx, devs, sem):
        i2 = around(idx)[0]
        recv(sem + 2, part(i2, 0), devs[0])
        if two:
            recv(sem + 3, part(i2, 1), devs[1])

    xdev, zdev, ydev = (xp, xm), (zp, zm), (yp, ym)

    class Chunk:
        pass

    chunks = []
    for k, c in enumerate(s["chunks"]):
        ch = Chunk()
        ch.k, ch.sem = k, k * SEMS
        for name, ref in c.items():
            setattr(ch, name, ref)
        ch.xb, ch.zb = ch.own.shape[1], ch.g.shape[3]
        unit = 8 if k == 0 else 16
        ch.xa, ch.xc = halves(ch.xb, unit)
        ch.za, ch.zc = halves(ch.zb, unit)
        ch.f = None if k == 0 else ORDER[k - 1]
        chunks.append(ch)

    waited = set()

    def load_wait(*part):
        if part not in waited:
            waited.add(part)
            loads[part].wait()

    rows_c = bv[0].shape[1] // 4
    mine = pl.ds(pl.multiple_of(ctx * rows_c, rows_c), rows_c)

    def stage_core():
        ch = chunks[0]
        for f in ORDER:
            load_wait("w", f)
            load_wait("b", f)
            s["cfull"][f] = lax.dot_general(
                bv[f][...], wv[f][...], (((0,), (0,)), ((), ())), preferred_element_type=jnp.float32)
        part = s["cpart"]
        for f in range(3):
            part[f // 2, (f % 2) * 2:(f % 2) * 2 + 2] = s["cfull"][f, mine].reshape(2, ch.xb, -1)
        part[1, 2:4] = jnp.zeros_like(part[1, 2:4])
        for q, i in enumerate(around(xi)):
            send(ch.sem + q, part.at[1 - core, i], ch.cr.at[i], partner)
        for i in range(4):
            ch.own[i] = part[core, i]

    def tile_probe(f, row, dst):
        rows = dst.shape[0]
        where = pl.ds(pl.multiple_of(row, rows), rows)
        if turned[f]:
            dst[...] = lax.dot_general(
                xv[f][:, where], wv[f][...], (((0,), (0,)), ((), ())),
                preferred_element_type=jnp.float32)
        else:
            dst[...] = jnp.dot(xv[f][where], wv[f][...], preferred_element_type=jnp.float32)

    def stage_probe(ch):
        load_wait("w", ch.f)
        load_wait("x", ch.f, 0)
        for q, i in enumerate(around(xi)):
            tile_probe(ch.f, (1 - core) * half + i * ch.xb, ch.cs.at[i])
            send(ch.sem + q, ch.cs.at[i], ch.cr.at[i], partner)
        load_wait("x", ch.f, 1)
        for i in around(xi):
            tile_probe(ch.f, core * half + i * ch.xb, ch.own.at[i])

    def stage_a(ch):
        def pre(i, q):
            recv(ch.sem + q, ch.cr.at[i], partner)
            ch.own[i] = ch.own[i] + ch.cr[i]
        rs_start(ch.own, ch.xr1, ch.xr2, ch.xa, ch.xc, xi, xdev, ch.sem + 4, pre)

    def stage_b(ch):
        rs_mid(ch.own, ch.xr1, ch.xr2, ch.xa, ch.xc, xi, xdev, ch.sem + 4)

    def stage_d(ch):
        rs_end(ch.xr2, ch.xa, ch.xc, xdev, ch.sem + 4)

        def pre(i, q):
            rows = pl.ds(pl.multiple_of(i * ch.zb, ch.zb), ch.zb)
            ch.zs[i] = ch.own[xi, rows] + ch.xr2[0, rows] + ch.xr2[1, rows]
        rs_start(ch.zs, ch.zr1, ch.zr2, ch.za, ch.zc, zi, zdev, ch.sem + 10, pre)

    def stage_e(ch):
        rs_mid(ch.zs, ch.zr1, ch.zr2, ch.za, ch.zc, zi, zdev, ch.sem + 10)

    def zblock(ch):
        return lambda i: ch.g.at[core, xi, i]

    def zpart(ch):
        return lambda i, h: ch.g.at[core, xi, i, (0 if h == 0 else ch.za):(ch.za if h == 0 else ch.zb)]

    def xblock(ch):
        return lambda i: ch.g.at[core, i]

    def xpart(ch):
        return lambda i, h: ch.g.at[core, i, 2 * h:2 * h + 2]

    def stage_f(ch):
        rs_end(ch.zr2, ch.za, ch.zc, zdev, ch.sem + 10)
        ch.g[core, xi, zi] = (ch.zs[zi] + ch.zr2[0] + ch.zr2[1]).astype(ch.g.dtype)
        ag_start(zblock(ch), zi, zdev, ch.sem + 16)

    def stage_g(ch):
        ag_mid(zblock(ch), zpart(ch), ch.zc > 0, zi, zdev, ch.sem + 16)

    def forward(ch):
        def got(i, q):
            send(ch.sem + 24 + q, ch.g.at[core, i], ch.g.at[core, i], partner)
        return got

    def stage_h(ch):
        ag_end(zpart(ch), ch.zc > 0, zi, zdev, ch.sem + 16)
        ag_start(xblock(ch), xi, xdev, ch.sem + 20)
        forward(ch)(xi, 0)

    def stage_i(ch):
        ag_mid(xblock(ch), xpart(ch), True, xi, xdev, ch.sem + 20, forward(ch))

    def stage_j(ch):
        ag_end(xpart(ch), True, xi, xdev, ch.sem + 20)
        i2, ip, im, me = around(xi)
        forward(ch)(i2, 3)
        for q, i in enumerate((me, im, ip, i2)):
            recv(ch.sem + 24 + q, ch.g.at[1 - core, i], partner)

    def stage_prior():
        g = chunks[0].g
        for f in ORDER:
            load_wait("e", f)
            pair = g[f // 2, (f % 2) * 2:(f % 2) * 2 + 2].reshape(rows_c, -1)
            row = lax.broadcasted_iota(jnp.int32, pair.shape, 0) + ctx * rows_c
            col = lax.broadcasted_iota(jnp.int32, pair.shape, 1)
            eig = jnp.sum(jnp.where(row == col, ev[f][...], 0.0), axis=1, keepdims=True)
            weighted = pair * (0.9 * eig)
            high = weighted.astype(jnp.bfloat16)
            low = (weighted - high.astype(jnp.float32)).astype(jnp.bfloat16)
            wp = s["wp"]
            wp[0] = jnp.zeros_like(wp[0])
            wp[1] = jnp.zeros_like(wp[1])
            wp[0, mine] = high
            wp[1, mine] = low
            d = s["d"][f]
            rows = d.shape[0]
            for r in range(0, rows, 256):
                n = min(256, rows - r)
                b = bv[f][r:r + n]
                d[r:r + n] = (jnp.dot(b, wp[0], preferred_element_type=jnp.float32)
                              + jnp.dot(b, wp[1], preferred_element_type=jnp.float32))

    def stage_t(f):
        if turned[f]:
            return
        rows = xv[f].shape[1]

        @pl.loop(0, tokens // 256)
        def _(t):
            cols = pl.ds(pl.multiple_of(t * 256, 256), 256)
            for r in range(0, rows, 256):
                n = min(256, rows - r)
                s["xt"][f][r:r + n, cols] = xv[f][cols, r:r + n].T

    def stage_k(ch):
        f, d = ch.f, s["d"][ch.f]
        z = ch.g[...].reshape(tokens, -1)
        xt = xv[f] if turned[f] else s["xt"][f]
        rows = d.shape[0]
        for r in range(0, rows, 256):
            n = min(256, rows - r)
            d[r:r + n] = d[r:r + n] + (0.1 / total) * jnp.dot(
                xt[r:r + n], z, preferred_element_type=jnp.float32)
        dp, fb = s["dp"][f], rows // 4
        for i in range(4):
            dp[i, 0:fb] = d[i * fb:(i + 1) * fb]
        n = dp.shape[1]
        ch.ya, ch.yc = halves(n, 8)
        rs_start(dp, s["yr1"][f], s["yr2"][f], ch.ya, ch.yc, ctx, ydev, ch.sem + 28, lambda i, q: None)

    def stage_l(ch):
        f = ch.f
        rs_mid(s["dp"][f], s["yr1"][f], s["yr2"][f], ch.ya, ch.yc, ctx, ydev, ch.sem + 28)

    def stage_m(ch):
        f = ch.f
        rs_end(s["yr2"][f], ch.ya, ch.yc, ydev, ch.sem + 28)
        n = outs[f].shape[0]
        r2 = s["yr2"][f]
        outs[f][...] = s["dp"][f][ctx, 0:n] + r2[0, 0:n] + r2[1, 0:n]

    for f in range(3):
        dp = s["dp"][f]
        n = outs[f].shape[0]
        if dp.shape[1] != n:
            dp[...] = jnp.zeros_like(dp)

    c0, c1, c2, c3 = chunks
    events = [
        (0.0, lambda: stage_probe(c1)), (3.0, lambda: stage_a(c1)),
        (3.1, stage_core), (3.2, lambda: stage_probe(c2)), (3.3, lambda: stage_a(c0)),
        (3.4, lambda: stage_probe(c3)), (40.0, None),
    ]
    times = {"b": 4.5, "d": 10, "e": 13, "f": 16, "g": 18.5, "h": 21, "i": 27, "j": 30, "k": 30.1,
             "l": 33.5, "m": 37}
    stages = {"b": stage_b, "d": stage_d, "e": stage_e, "f": stage_f, "g": stage_g, "h": stage_h,
              "i": stage_i, "j": stage_j, "k": stage_k, "l": stage_l, "m": stage_m}
    for ch, t0 in ((c0, 5.0), (c1, 3.0), (c2, 9.0), (c3, 17.0)):
        if ch.k >= 2:
            events.append((t0 - 0.4, lambda ch=ch: stage_a(ch)))
        for name, t in times.items():
            if ch.k == 0 and name in "klm":
                continue
            events.append((t0 + t, lambda ch=ch, name=name: stages[name](ch)))
    events.append((8.7, lambda: stage_t(ORDER[0])))
    events.append((17.2, lambda: stage_t(ORDER[1])))
    events.append((17.3, lambda: stage_t(ORDER[2])))
    events = [e for e in events if e[1] is not None]
    prior_at = max(5.0 + times["j"], 0) + 0.01
    down_k = 3.0 + times["k"]
    events = [(t, fn) for t, fn in events]
    events.append((min(prior_at, 1e9), stage_prior))
    events = [(t + (prior_at - down_k + 0.02 if prior_at > down_k and t >= down_k and t < prior_at
                    and fn is not stage_prior and t == down_k else 0), fn) for t, fn in events]
    for _, fn in sorted(events, key=lambda e: e[0]):
        fn()

    for copy in pending:
        copy.wait_send()


def sketch(total, xs, ws, bs, es):
    tokens = xs[0].shape[0]
    r = ws[0].shape[1]
    f32, bf16 = jnp.float32, jnp.bfloat16
    vm = pltpu.VMEM

    def chunk(h, dtype, first):
        xb, zb = h // 4, h // 16
        unit = 8 if first else 16
        xa, za = halves(xb, unit)[0], halves(zb, unit)[0]
        c = dict(
            own=vm((4, xb, r), f32), cr=vm((4, xb, r), f32), zs=vm((4, zb, r), f32),
            xr1=vm((2, xa, r), f32), xr2=vm((2, xb, r), f32),
            zr1=vm((2, za, r), f32), zr2=vm((2, zb, r), f32), g=vm((2, 4, 4, zb, r), dtype),
        )
        if not first:
            c["cs"] = vm((4, xb, r), f32)
        return c

    fs = [x.shape[1] for x in xs]
    turned = [f % 128 != 0 for f in fs]
    xs = [x.T if turn else x for x, turn in zip(xs, turned)]
    fb = [-(-(f // 4) // 8) * 8 for f in fs]
    scratch = dict(
        chunks=[chunk(r // 2, f32, True)] + [chunk(tokens // 2, bf16, False) for _ in range(3)],
        xv=[vm(x.shape, bf16) for x in xs], wv=[vm((f, r), bf16) for f in fs],
        bv=[vm((f, r), bf16) for f in fs], ev=[vm((1, r), f32) for f in fs],
        xt=[vm((8, 128) if turn else (f, tokens), bf16) for f, turn in zip(fs, turned)], d=[vm((f, r), f32) for f in fs],
        dp=[vm((4, n, r), f32) for n in fb], yr1=[vm((2, halves(n, 8)[0], r), f32) for n in fb],
        yr2=[vm((2, n, r), f32) for n in fb],
        cfull=vm((3, r, r), f32), cpart=vm((2, 4, r // 8, r), f32), wp=vm((2, r, r), bf16),
        ssem=pltpu.SemaphoreType.DMA((4 * SEMS,)), rsem=pltpu.SemaphoreType.DMA((4 * SEMS,)),
        lsem=pltpu.SemaphoreType.DMA((15,)),
    )

    def body(*refs):
        sketch_kernel(total, tokens, turned, *refs)

    return pl.pallas_call(
        body,
        out_shape=[jax.ShapeDtypeStruct((f // 4, r), f32) for f in fs],
        in_specs=[pl.BlockSpec(memory_space=pl.ANY)] * 12,
        out_specs=[pl.BlockSpec(memory_space=pltpu.VMEM)] * 3,
        scratch_shapes=(scratch,),
        compiler_params=pltpu.CompilerParams(
            collective_id=0, has_side_effects=True, vmem_limit_bytes=60 * 2**20),
        name="sketch",
    )(*xs, *ws, *bs, *[e.reshape(1, r) for e in es])


def solution(mesh):
    def per_device(*args):
        total = args[0].shape[0] * mesh.shape["context"]
        return tuple(sketch(total, args[0:3], args[3:6], args[6:9], args[9:12]))

    rows = P(("section", "owner"), None)
    return jax.shard_map(
        per_device,
        mesh=mesh,
        in_specs=(P(("section", "context"), "owner"),) * 3 + (rows,) * 6 + (P("section"),) * 3,
        out_specs=(P(("section", "owner", "context"), None),) * 3,
        check_vma=False,
    )
```

time: 527 us -> 92.4 us (0.18)
  waiting for transfers between devices: 265 us -> 0 us
  blocking collectives: 215 us -> 0 us
  Pallas kernels: 0 us -> 86.4 us
  matrix products: 25.5 us -> 0 us
  between operations: 16.3 us -> 0.64 us
    psum x1 -> x0, waiting for transfers between devices: 265 us -> none  [per_device(): lax.psum((probes_local[0], probes_local[1], probes_local[2], cores_local[...]
    psum x1 -> x0, blocking collectives: 199 us -> none  [per_device(): lax.psum((probes_local[0], probes_local[1], probes_local[2], cores_local[...]
    pallas_call x0 -> x1, Pallas kernels: none -> 86.4 us  [sketch(): pl.pallas_call(body, out_shape=[jax.ShapeDtypeStruct((f // 4, r), f32) fo...]
    dot_general x12 -> x0, matrix products: 25.5 us -> none  [the longest x6 12.4 us: token_contract(): lax.dot_general(inputs, probe, (((0,), (0,)), ((), ())), preferred_elemen...]
    unnamed x1 -> x0, blocking collectives: 15.7 us -> none
  transfers between devices with their start and end apart: 4 -> 0, of which waited for: 1 -> 0; matrix products, arithmetic and copies ran while one was open for 6% -> 0% of each run, Pallas kernels for 0% -> 0%
where the time goes in v1:
time: 92.4 us; the launch traced here: 91.6 us
  Pallas kernels  86.4 us (94%)
  local copies, waits for them, and re-layouts  4.59 us (5%)
    pallas_call x1, Pallas kernels, sketch(): pl.pallas_call(body, out_shape=[jax.ShapeDtypeStruct((f // 4, r), f32) fo...  86.4 us
    unnamed x3, local copies, waits for them, and re-layouts  4.59 us

profile of v1, /device:TPU:1, one launch (start us, length us, event | category | flops | bytes accessed | tf_op | source)
XLA Modules:
  0.0 91.6 jit_solution(4958349259746320687)
XLA Ops:
  0.6 86.4 %sketch.1 = (f32[64,256]{1,0:T(8,128)}, f32[64,256]{1,0:T(8,128)}, f32[231,256]{1,0:T(8,128)}) custom-call(bf16[2048,256]{1,0:T(8,128)(2,1)} %refs_0_.1, bf16[2048,256]{1,0:T(8,128)(2,1)} %refs_1_.1, bf16[924,2048]{1,0:T(8,128)(2,1)} %bitcast.4, bf16[256,256]{1,0:T(8,128)(2,1)} %refs_3_.1, bf16[256,256]{1,0:T(8,128)(2,1)} %refs_4_.1, ...), custom_call_target="tpu_custom_call" | custom-call | tf_op jit(solution)/shard_map/sketch/pallas_call | solution.py:396
  87.0 1.5 %copy.18 = f32[64,256]{1,0:T(8,128)} copy(f32[64,256]{1,0:T(8,128)} %get-tuple-element.6) | data formatting | bytes 131072
  88.5 1.5 %copy.19 = f32[64,256]{1,0:T(8,128)} copy(f32[64,256]{1,0:T(8,128)} %get-tuple-element.7) | data formatting | bytes 131072
  90.0 1.6 %copy.20 = f32[231,256]{1,0:T(8,128)} copy(f32[231,256]{1,0:T(8,128)} %get-tuple-element.8) | data formatting | bytes 473088

commit v2 on v1

v2 whole, which is shorter than its diff:
```python
import jax
import jax.numpy as jnp
from jax import lax
from jax.experimental import pallas as pl
from jax.experimental.pallas import tpu as pltpu
from jax.sharding import PartitionSpec as P

PLAN = ((2, 2), (0, 2), (1, 2))
SEMS = 32
SCHEDULE = [
    "p1", "p0", "p2", "a0", "a1", "p3", "p4", "a2", "p5", "a3", "p6", "a4", "t0", "a5",
    "d0", "t1", "a6", "d1", "d2", "d3", "f0", "d4", "f1", "d5", "f2", "d6", "f3", "h0",
    "f4", "h1", "i0", "f5", "h2", "j0", "w0", "f6", "i1", "h3", "h4", "j1", "k1", "i2",
    "h5", "j2", "k2", "i3", "h6", "i4", "j3", "k3", "j4", "i5", "k4", "j5", "k5", "i6",
    "j6", "k6",
]
SPAN = 86.0
SCALE_ROWS = 16


def encode(src, dst):
    rows = src.shape[0]
    tiles = [(r, min(r + 64, rows)) for r in range(0, rows, 64)]
    top = None
    for lo, hi in tiles:
        peak = jnp.max(jnp.abs(src[lo:hi]), axis=0, keepdims=True)
        top = peak if top is None else jnp.maximum(top, peak)
    scale = (top * 1.01 + 1e-30).astype(jnp.bfloat16)
    base = dst.shape[0] - SCALE_ROWS
    dst[base:base + SCALE_ROWS] = jnp.broadcast_to(scale, (SCALE_ROWS, src.shape[1]))
    slope = (2.0 * SPAN) / dst[base:base + SCALE_ROWS].astype(jnp.float32)[0:1]
    for lo, hi in tiles:
        v = src[lo:hi]
        y = jnp.exp(jnp.abs(v) * slope - SPAN)
        dst[lo:hi] = jnp.where(v < 0, -y, y).astype(jnp.bfloat16)


def decode(src, r, n):
    base = src.shape[0] - SCALE_ROWS
    slope = src[base:base + SCALE_ROWS].astype(jnp.float32)[0:1] * (0.5 / SPAN)
    y = src[pl.ds(r, n)].astype(jnp.float32)
    v = (jnp.log(jnp.abs(y)) + SPAN) * slope
    return jnp.where(y < 0, -v, v)


def sketch_kernel(total, tokens, turned, *refs):
    xs, ws, bs, es, outs = refs[0:3], refs[3:6], refs[6:9], refs[9:12], refs[12:15]
    s = refs[15]
    ssem, rsem, lsem = s["ssem"], s["rsem"], s["lsem"]
    owner, ctx = lax.axis_index("owner"), lax.axis_index("context")
    core, zi, xi = lax.rem(owner, 2), lax.rem(lax.div(owner, 2), 4), lax.div(owner, 8)

    def at(x, z, c):
        return {"owner": (lax.rem(x, 4) * 4 + lax.rem(z, 4)) * 2 + c}

    partner = at(xi, zi, 1 - core)
    hops = (2, 1, 3)
    xdev = [at(xi + h, zi, core) for h in hops]
    zdev = [at(xi, zi + h, core) for h in hops]
    ydev = [{"context": lax.rem(ctx + h, 4)} for h in hops]

    pending = []

    def remote(i, src, dst, dev):
        return pltpu.make_async_remote_copy(
            src_ref=src, dst_ref=dst, send_sem=ssem.at[i], recv_sem=rsem.at[i],
            device_id=dev, device_id_type=pl.DeviceIdType.MESH,
        )

    def send(i, src, dst, dev):
        copy = remote(i, src, dst, dev)
        copy.start()
        pending.append(copy)

    def recv(i, dst, dev):
        remote(i, dst, dst, dev).wait_recv()

    half = tokens // 2
    xv, wv, bv, ev = s["xv"], s["wv"], s["bv"], s["ev"]
    factors = [f for f, _ in PLAN]
    loads = {}
    for f in factors:
        loads["w", f] = pltpu.make_async_copy(ws[f], wv[f], lsem.at[f])
        for q, c in enumerate((1 - core, core)):
            rows = pl.ds(pl.multiple_of(c * half, half), half)
            where = (slice(None), rows) if turned[f] else rows
            loads["x", f, q] = pltpu.make_async_copy(
                xs[f].at[where], xv[f].at[where], lsem.at[3 + 2 * f + q])
        loads["b", f] = pltpu.make_async_copy(bs[f], bv[f], lsem.at[9 + f])
        loads["e", f] = pltpu.make_async_copy(es[f], ev[f], lsem.at[12 + f])
    first = factors[0]
    order = [("w", first), ("x", first, 0), ("x", first, 1)]
    order += [("w", f) for f in factors[1:]] + [("b", f) for f in factors]
    order += [("x", f, q) for f in factors[1:] for q in (0, 1)] + [("e", f) for f in factors]
    for part in order:
        loads[part].start()

    barrier = pltpu.get_barrier_semaphore()
    peers = [partner] + xdev + zdev + ydev
    for dev in peers:
        pl.semaphore_signal(barrier, inc=1, device_id=dev, device_id_type=pl.DeviceIdType.MESH)

    waited = set()

    def load_wait(*part):
        if part not in waited:
            waited.add(part)
            loads[part].wait()

    def around(i):
        return [lax.rem(i + h, 4) for h in hops]

    class Chunk:
        pass

    chunks = []
    for k, c in enumerate(s["chunks"]):
        ch = Chunk()
        ch.k, ch.sem = k, k * SEMS
        for name, ref in c.items():
            setattr(ch, name, ref)
        ch.xb, ch.zb = ch.own.shape[1], ch.g.shape[3]
        chunks.append(ch)
    k = 1
    for f, pieces in PLAN:
        for piece in range(pieces):
            chunks[k].f, chunks[k].t0, chunks[k].last = f, piece * (half // pieces), piece == pieces - 1
            k += 1

    rows_c = bv[0].shape[1] // 4
    mine = pl.ds(pl.multiple_of(ctx * rows_c, rows_c), rows_c)

    def stage_core():
        ch = chunks[0]
        part = s["cpart"]
        for f in factors:
            load_wait("w", f)
            load_wait("b", f)
            s["cfull"][...] = lax.dot_general(
                bv[f][...], wv[f][...], (((0,), (0,)), ((), ())), preferred_element_type=jnp.float32)
            part[f // 2, (f % 2) * 2:(f % 2) * 2 + 2] = s["cfull"][mine].reshape(2, ch.xb, -1)
        part[1, 2:4] = jnp.zeros_like(part[1, 2:4])
        for q, i in enumerate(around(xi) + [xi]):
            send(ch.sem + q, part.at[1 - core, i], ch.cr.at[i], partner)
        for i in range(4):
            ch.own[i] = part[core, i]

    def tile_probe(f, row, dst):
        rows = dst.shape[0]
        where = pl.ds(pl.multiple_of(row, rows), rows)
        if turned[f]:
            dst[...] = lax.dot_general(
                xv[f][:, where], wv[f][...], (((0,), (0,)), ((), ())),
                preferred_element_type=jnp.float32)
        else:
            dst[...] = jnp.dot(xv[f][where], wv[f][...], preferred_element_type=jnp.float32)

    def stage_probe(ch, after_first=None):
        load_wait("w", ch.f)
        load_wait("x", ch.f, 0)
        for q, i in enumerate(around(xi) + [xi]):
            tile_probe(ch.f, (1 - core) * half + ch.t0 + i * ch.xb, ch.cs.at[i])
            if q == 0 and after_first:
                after_first()
            send(ch.sem + q, ch.cs.at[i], ch.cr.at[i], partner)
        load_wait("x", ch.f, 1)
        for i in around(xi) + [xi]:
            tile_probe(ch.f, core * half + ch.t0 + i * ch.xb, ch.own.at[i])

    def stage_a(ch):
        for q, i in enumerate(around(xi) + [xi]):
            recv(ch.sem + q, ch.cr.at[i], partner)
            ch.own[i] = ch.own[i] + ch.cr[i]
            if q < 3:
                if ch.k == 0:
                    send(ch.sem + 4 + q, ch.own.at[i], ch.xr.at[q], xdev[q])
                else:
                    encode(ch.own.at[i], ch.xs.at[q])
                    send(ch.sem + 4 + q, ch.xs.at[q], ch.xr.at[q], xdev[q])

    def stage_d(ch):
        for q in (1, 2, 0):
            recv(ch.sem + 4 + q, ch.xr.at[q], xdev[q])
        for q, i in enumerate(around(zi) + [zi]):
            r = pl.multiple_of(i * ch.zb, ch.zb)
            rows = pl.ds(r, ch.zb)
            v = ch.own[xi, rows]
            for p in range(3):
                v = v + (ch.xr[p, rows] if ch.k == 0 else decode(ch.xr.at[p], r, ch.zb))
            ch.zs[i] = v
            if q < 3 and ch.k == 0:
                send(ch.sem + 7 + q, ch.zs.at[i], ch.zr.at[q], zdev[q])
            elif q < 3:
                encode(ch.zs.at[i], ch.zx.at[q])
                send(ch.sem + 7 + q, ch.zx.at[q], ch.zr.at[q], zdev[q])

    def stage_f(ch):
        for q in (1, 2, 0):
            recv(ch.sem + 7 + q, ch.zr.at[q], zdev[q])
        v = ch.zs[zi]
        for p in range(3):
            v = v + (ch.zr[p] if ch.k == 0 else decode(ch.zr.at[p], 0, ch.zb))
        ch.g[core, xi, zi] = v.astype(ch.g.dtype)
        for q in range(3):
            block = ch.g.at[core, xi, zi]
            send(ch.sem + 10 + q, block, block, zdev[q])

    def source(i, q):
        return lax.rem(i + 4 - hops[q], 4)

    def forward(ch, q, i):
        send(ch.sem + 16 + q, ch.g.at[core, i], ch.g.at[core, i], partner)

    def stage_h(ch):
        for q in (1, 2, 0):
            recv(ch.sem + 10 + q, ch.g.at[core, xi, source(zi, q)], zdev[q])
        for q in range(3):
            block = ch.g.at[core, xi]
            send(ch.sem + 13 + q, block, block, xdev[q])
        forward(ch, 3, xi)

    def stage_i(ch):
        for q in (1, 2, 0):
            recv(ch.sem + 13 + q, ch.g.at[core, source(xi, q)], xdev[q])
            forward(ch, q, source(xi, q))

    def stage_j(ch):
        for q in (3, 1, 2, 0):
            i = xi if q == 3 else source(xi, q)
            recv(ch.sem + 16 + q, ch.g.at[1 - core, i], partner)

    begun = set()

    def add(f, r, n, value):
        d = s["d"][f]
        d[r:r + n] = d[r:r + n] + value if f in begun else value

    def stage_prior():
        g = chunks[0].g
        for f in factors:
            load_wait("e", f)
            pair = g[f // 2, (f % 2) * 2:(f % 2) * 2 + 2].reshape(rows_c, -1)
            row = lax.broadcasted_iota(jnp.int32, pair.shape, 0) + ctx * rows_c
            col = lax.broadcasted_iota(jnp.int32, pair.shape, 1)
            eig = jnp.sum(jnp.where(row == col, ev[f][...], 0.0), axis=1, keepdims=True)
            weighted = pair * (0.9 * eig)
            high = weighted.astype(jnp.bfloat16)
            low = (weighted - high.astype(jnp.float32)).astype(jnp.bfloat16)
            wp = s["wp"]
            wp[0] = jnp.zeros_like(wp[0])
            wp[1] = jnp.zeros_like(wp[1])
            wp[0, mine] = high
            wp[1, mine] = low
            rows = s["d"][f].shape[0]
            for r in range(0, rows, 256):
                n = min(256, rows - r)
                b = bv[f][r:r + n]
                add(f, r, n, jnp.dot(b, wp[0], preferred_element_type=jnp.float32)
                    + jnp.dot(b, wp[1], preferred_element_type=jnp.float32))
            begun.add(f)

    def stage_t(f):
        if turned[f]:
            return
        load_wait("x", f, 0)
        load_wait("x", f, 1)
        rows = xv[f].shape[1]

        @pl.loop(0, tokens // 256)
        def _(t):
            cols = pl.ds(pl.multiple_of(t * 256, 256), 256)
            for r in range(0, rows, 256):
                n = min(256, rows - r)
                s["xt"][f][r:r + n, cols] = xv[f][cols, r:r + n].T

    def stage_k(ch):
        f, d = ch.f, s["d"][ch.f]
        xt = xv[f] if turned[f] else s["xt"][f]
        rows, h = d.shape[0], 4 * ch.xb
        z = [ch.g[c].reshape(h, -1) for c in (0, 1)]
        for r in range(0, rows, 256):
            n = min(256, rows - r)
            value = [jnp.dot(xt[r:r + n, c * half + ch.t0:c * half + ch.t0 + h], z[c],
                             preferred_element_type=jnp.float32) for c in (0, 1)]
            add(f, r, n, (0.1 / total) * (value[0] + value[1]))
        begun.add(f)
        if not ch.last:
            return
        dp, fb = s["dp"][f], rows // 4
        for i in range(4):
            dp[i, 0:fb] = d[i * fb:(i + 1) * fb]
        yx, yr = s["yx"][f], s["yr"][f]
        for q, i in enumerate(around(ctx)):
            encode(dp.at[i], yx.at[q])
            send(ch.sem + 20 + q, yx.at[q], yr.at[q], ydev[q])

    def stage_m(ch):
        if not ch.last:
            return
        f = ch.f
        for q in (1, 2, 0):
            recv(ch.sem + 20 + q, s["yr"][f].at[q], ydev[q])
        n = outs[f].shape[0]
        yr = s["yr"][f]
        v = s["dp"][f][ctx]
        for p in range(3):
            v = v + decode(yr.at[p], 0, v.shape[0])
        outs[f][...] = v[0:n]

    def entry():
        for f in factors:
            dp = s["dp"][f]
            if dp.shape[1] != outs[f].shape[0]:
                dp[...] = jnp.zeros_like(dp)
        pl.semaphore_wait(barrier, len(peers))

    stages = {"a": stage_a, "d": stage_d, "f": stage_f, "h": stage_h, "i": stage_i, "j": stage_j, "k": stage_k}
    for step in SCHEDULE:
        name, k = step[0], int(step[1:])
        if name == "p" and k == 0:
            stage_core()
        elif name == "p":
            stage_probe(chunks[k], entry if k == 1 else None)
        elif name == "t":
            stage_t(k)
        elif name == "w":
            stage_prior()
        else:
            stages[name](chunks[k])
    for ch in chunks[1:]:
        stage_m(ch)

    for copy in pending:
        copy.wait_send()


def sketch(total, xs, ws, bs, es):
    tokens = xs[0].shape[0]
    r = ws[0].shape[1]
    f32, bf16 = jnp.float32, jnp.bfloat16
    vm = pltpu.VMEM

    def chunk(h, dtype, first):
        xb, zb = h // 4, h // 16
        def message(n):
            return vm((3, n, r), f32) if first else vm((3, n + SCALE_ROWS, r), bf16)
        c = dict(
            own=vm((4, xb, r), f32), cr=vm((4, xb, r), f32), zs=vm((4, zb, r), f32),
            xr=message(xb), zr=message(zb), g=vm((2, 4, 4, zb, r), dtype),
        )
        if not first:
            c["cs"] = vm((4, xb, r), f32)
            c["xs"], c["zx"] = message(xb), message(zb)
        return c

    fs = [x.shape[1] for x in xs]
    turned = [f % 128 != 0 for f in fs]
    xs = [x.T if turn else x for x, turn in zip(xs, turned)]
    fb = [-(-(f // 4) // 8) * 8 for f in fs]
    message_rows = [-(-n // 16) * 16 + SCALE_ROWS for n in fb]
    pieces = [n for _, n in PLAN for _ in range(n)]
    count = SEMS * (1 + len(pieces))
    scratch = dict(
        chunks=[chunk(r // 2, f32, True)] + [chunk(tokens // 2 // n, bf16, False) for n in pieces],
        xv=[vm(x.shape, bf16) for x in xs], wv=[vm((f, r), bf16) for f in fs],
        bv=[vm((f, r), bf16) for f in fs], ev=[vm((1, r), f32) for f in fs],
        xt=[vm((8, 128) if turn else (f, tokens), bf16) for f, turn in zip(fs, turned)],
        d=[vm((f, r), f32) for f in fs],
        dp=[vm((4, n, r), f32) for n in fb], yr=[vm((3, n, r), bf16) for n in message_rows],
        yx=[vm((3, n, r), bf16) for n in message_rows],
        cfull=vm((r, r), f32), cpart=vm((2, 4, r // 8, r), f32), wp=vm((2, r, r), bf16),
        ssem=pltpu.SemaphoreType.DMA((count,)), rsem=pltpu.SemaphoreType.DMA((count,)),
        lsem=pltpu.SemaphoreType.DMA((15,)),
    )

    def body(*refs):
        sketch_kernel(total, tokens, turned, *refs)

    return pl.pallas_call(
        body,
        out_shape=[jax.ShapeDtypeStruct((f // 4, r), f32) for f in fs],
        in_specs=[pl.BlockSpec(memory_space=pltpu.HBM)] * 12,
        out_specs=[pl.BlockSpec(memory_space=pltpu.VMEM)] * 3,
        scratch_shapes=(scratch,),
        compiler_params=pltpu.CompilerParams(
            collective_id=0, has_side_effects=True, vmem_limit_bytes=60 * 2**20),
        name="sketch",
    )(*xs, *ws, *bs, *[e.reshape(1, r) for e in es])


def place(*values):
    def body(*refs):
        for src, dst in zip(refs[:3], refs[3:]):
            dst[...] = src[...]

    return pl.pallas_call(
        body,
        out_shape=tuple(jax.ShapeDtypeStruct(v.shape, v.dtype) for v in values),
        compiler_params=pltpu.CompilerParams(vmem_limit_bytes=2 * 2**20),
        name="place",
    )(*values)


def solution(mesh):
    def per_device(*args):
        total = args[0].shape[0] * mesh.shape["context"]
        return place(*sketch(total, args[0:3], args[3:6], args[6:9], args[9:12]))

    rows = P(("section", "owner"), None)
    return jax.shard_map(
        per_device,
        mesh=mesh,
        in_specs=(P(("section", "context"), "owner"),) * 3 + (rows,) * 6 + (P("section"),) * 3,
        out_specs=(P(("section", "owner", "context"), None),) * 3,
        check_vma=False,
    )
```

time: 92.4 us -> 73.8 us (0.80)
  Pallas kernels: 86.4 us -> 70.3 us
  local copies, waits for them, and re-layouts: 4.59 us -> 2.61 us
    pallas_call x1, Pallas kernels: 86.4 us -> 69.6 us  [sketch(): pl.pallas_call(body, out_shape=[jax.ShapeDtypeStruct((f // 4, r), f32) fo...]
    unnamed x3 -> x6, local copies, waits for them, and re-layouts: 4.59 us -> 2.61 us
where the time goes in v2:
time: 73.8 us; the launch traced here: 73.6 us
  Pallas kernels  70.3 us (95%)
  local copies, waits for them, and re-layouts  2.61 us (4%)
    pallas_call x1, Pallas kernels, sketch(): pl.pallas_call(body, out_shape=[jax.ShapeDtypeStruct((f // 4, r), f32) fo...  69.6 us
    unnamed x6, local copies, waits for them, and re-layouts  2.61 us

profile of v2, /device:TPU:1, one launch (start us, length us, event | category | flops | bytes accessed | tf_op | source)
XLA Modules:
  0.0 73.6 jit_solution(2032045207033478966)
XLA Ops:
  0.6 69.6 %sketch.1 = (f32[64,256]{1,0:T(8,128)}, f32[64,256]{1,0:T(8,128)}, f32[231,256]{1,0:T(8,128)}) custom-call(bf16[2048,256]{1,0:T(8,128)(2,1)} %refs_0_.1, bf16[2048,256]{1,0:T(8,128)(2,1)} %refs_1_.1, bf16[924,2048]{1,0:T(8,128)(2,1)} %bitcast.4, bf16[256,256]{1,0:T(8,128)(2,1)} %refs_3_.1, bf16[256,256]{1,0:T(8,128)(2,1)} %refs_4_.1, ...), custom_call_target="tpu_custom_call" | custom-call | tf_op jit(solution)/shard_map/sketch/pallas_call | solution.py:379
  70.2 0.0 copy-start
  70.2 0.9 %copy-done = f32[231,256]{1,0:T(8,128)S(1)} copy-done((f32[231,256]{1,0:T(8,128)S(1)}, f32[231,256]{1,0:T(8,128)}, u32[]{:S(2)}) %copy-start) | copy-done | bytes 236568
  71.1 0.0 copy-start.1
  71.1 0.8 %copy-done.1 = f32[64,256]{1,0:T(8,128)S(1)} copy-done((f32[64,256]{1,0:T(8,128)S(1)}, f32[64,256]{1,0:T(8,128)}, u32[]{:S(2)}) %copy-start.1) | copy-done | bytes 65560
  72.0 0.0 copy-start.2
  72.0 0.8 %copy-done.2 = f32[64,256]{1,0:T(8,128)S(1)} copy-done((f32[64,256]{1,0:T(8,128)S(1)}, f32[64,256]{1,0:T(8,128)}, u32[]{:S(2)}) %copy-start.2) | copy-done | bytes 65560
  72.8 0.8 %place.1 = (f32[64,256]{1,0:T(8,128)}, f32[64,256]{1,0:T(8,128)}, f32[231,256]{1,0:T(8,128)}) custom-call(f32[64,256]{1,0:T(8,128)S(1)} %copy-done.1, f32[64,256]{1,0:T(8,128)S(1)} %copy-done.2, f32[231,256]{1,0:T(8,128)S(1)} %copy-done), custom_call_target="tpu_custom_call" | custom-call | tf_op jit(solution)/shard_map/place/pallas_call | solution.py:396
Async XLA Ops:
  70.2 0.9 %copy-start = (f32[231,256]{1,0:T(8,128)S(1)}, f32[231,256]{1,0:T(8,128)}, u32[]{:S(2)}) copy-start(f32[231,256]{1,0:T(8,128)} %get-tuple-element.8.refs_2_) | copy-start | bytes 709636
  71.1 0.8 %copy-start.1 = (f32[64,256]{1,0:T(8,128)S(1)}, f32[64,256]{1,0:T(8,128)}, u32[]{:S(2)}) copy-start(f32[64,256]{1,0:T(8,128)} %get-tuple-element.6.refs_0_) | copy-start | bytes 196612
  72.0 0.8 %copy-start.2 = (f32[64,256]{1,0:T(8,128)S(1)}, f32[64,256]{1,0:T(8,128)}, u32[]{:S(2)}) copy-start(f32[64,256]{1,0:T(8,128)} %get-tuple-element.7.refs_1_) | copy-start | bytes 196612

commit v3 on v2

--- a/solution.py
+++ b/solution.py
@@ -5,17 +5,18 @@
 from jax.experimental.pallas import tpu as pltpu
 from jax.sharding import PartitionSpec as P
 
-PLAN = ((2, 2), (0, 2), (1, 2))
+PLAN = ((2, 4, 0), (2, 4, 0), (0, 4, 0), (0, 4, 0), (1, 4, 0), (1, 2, 0), (1, 2, 1))
 SEMS = 32
 SCHEDULE = [
-    "p1", "p0", "p2", "a0", "a1", "p3", "p4", "a2", "p5", "a3", "p6", "a4", "t0", "a5",
-    "d0", "t1", "a6", "d1", "d2", "d3", "f0", "d4", "f1", "d5", "f2", "d6", "f3", "h0",
-    "f4", "h1", "i0", "f5", "h2", "j0", "w0", "f6", "i1", "h3", "h4", "j1", "k1", "i2",
-    "h5", "j2", "k2", "i3", "h6", "i4", "j3", "k3", "j4", "i5", "k4", "j5", "k5", "i6",
-    "j6", "k6",
+    "p1", "p0", "s0", "s1", "p2", "s2", "p3", "s3", "a0", "p4", "s4", "a1", "p5", "s5",
+    "a2", "p6", "s6", "a3", "p7", "s7", "t0", "a4", "a5", "d0", "t1", "a6", "a7", "d1",
+    "d2", "f0", "d3", "d7", "d4", "f1", "g0", "f2", "d5", "h0", "d6", "f3", "f7", "f4",
+    "g1", "i0", "h1", "g2", "j0", "w0", "h2", "g7", "h7", "f5", "f6", "g3", "i1", "h3",
+    "j1", "i2", "g4", "k1", "h4", "j2", "k2", "i3", "g5", "i7", "g6", "h5", "h6", "i4",
+    "j3", "k3", "j7", "k7", "j4", "k4", "i5", "i6", "j5", "k5", "j6", "k6",
 ]
 SPAN = 86.0
-SCALE_ROWS = 16
+SCALE_ROWS = 8
 
 
 def encode(src, dst):
@@ -77,7 +78,7 @@
 
     half = tokens // 2
     xv, wv, bv, ev = s["xv"], s["wv"], s["bv"], s["ev"]
-    factors = [f for f, _ in PLAN]
+    factors = list(dict.fromkeys(f for f, _, _ in PLAN))
     loads = {}
     for f in factors:
         loads["w", f] = pltpu.make_async_copy(ws[f], wv[f], lsem.at[f])
@@ -121,11 +122,16 @@
             setattr(ch, name, ref)
         ch.xb, ch.zb = ch.own.shape[1], ch.g.shape[3]
         chunks.append(ch)
-    k = 1
-    for f, pieces in PLAN:
-        for piece in range(pieces):
-            chunks[k].f, chunks[k].t0, chunks[k].last = f, piece * (half // pieces), piece == pieces - 1
-            k += 1
+    taken = dict.fromkeys(factors, 0)
+    for ch, (f, n, first_ring) in zip(chunks, ((None, 0, 0),) + PLAN):
+        x_ring, z_ring = (xi, xdev), (zi, zdev)
+        (ch.i1, ch.d1), (ch.i2, ch.d2) = (z_ring, x_ring) if first_ring else (x_ring, z_ring)
+        if f is not None:
+            ch.f, ch.t0 = f, taken[f] * half // 8
+            taken[f] += n
+    last = {chunks[int(step[1:])].f: int(step[1:]) for step in SCHEDULE if step[0] == "k"}
+    for ch in chunks[1:]:
+        ch.last = last[ch.f] == ch.k
 
     rows_c = bv[0].shape[1] // 4
     mine = pl.ds(pl.multiple_of(ctx * rows_c, rows_c), rows_c)
@@ -140,8 +146,6 @@
                 bv[f][...], wv[f][...], (((0,), (0,)), ((), ())), preferred_element_type=jnp.float32)
             part[f // 2, (f % 2) * 2:(f % 2) * 2 + 2] = s["cfull"][mine].reshape(2, ch.xb, -1)
         part[1, 2:4] = jnp.zeros_like(part[1, 2:4])
-        for q, i in enumerate(around(xi) + [xi]):
-            send(ch.sem + q, part.at[1 - core, i], ch.cr.at[i], partner)
         for i in range(4):
             ch.own[i] = part[core, i]
 
@@ -155,79 +159,98 @@
         else:
             dst[...] = jnp.dot(xv[f][where], wv[f][...], preferred_element_type=jnp.float32)
 
-    def stage_probe(ch, after_first=None):
+    def stage_probe(ch):
         load_wait("w", ch.f)
-        load_wait("x", ch.f, 0)
-        for q, i in enumerate(around(xi) + [xi]):
-            tile_probe(ch.f, (1 - core) * half + ch.t0 + i * ch.xb, ch.cs.at[i])
-            if q == 0 and after_first:
-                after_first()
-            send(ch.sem + q, ch.cs.at[i], ch.cr.at[i], partner)
-        load_wait("x", ch.f, 1)
-        for i in around(xi) + [xi]:
-            tile_probe(ch.f, core * half + ch.t0 + i * ch.xb, ch.own.at[i])
+        for q, c, blocks in ((0, 1 - core, ch.cs), (1, core, ch.own)):
+            load_wait("x", ch.f, q)
+            for i in range(4):
+                tile_probe(ch.f, c * half + ch.t0 + i * ch.xb, blocks.at[i])
+
+    entered = []
+
+    def stage_s(ch):
+        if not entered:
+            entered.append(entry())
+        for q, i in enumerate(around(ch.i1) + [ch.i1]):
+            src = s["cpart"].at[1 - core, i] if ch.k == 0 else ch.cs.at[i]
+            send(ch.sem + q, src, ch.cr.at[i], partner)
 
     def stage_a(ch):
-        for q, i in enumerate(around(xi) + [xi]):
+        for q, i in enumerate(around(ch.i1) + [ch.i1]):
             recv(ch.sem + q, ch.cr.at[i], partner)
             ch.own[i] = ch.own[i] + ch.cr[i]
             if q < 3:
-                if ch.k == 0:
-                    send(ch.sem + 4 + q, ch.own.at[i], ch.xr.at[q], xdev[q])
-                else:
-                    encode(ch.own.at[i], ch.xs.at[q])
-                    send(ch.sem + 4 + q, ch.xs.at[q], ch.xr.at[q], xdev[q])
+                src = ch.own.at[i]
+                if ch.k:
+                    encode(src, ch.xs.at[q])
+                    src = ch.xs.at[q]
+                send(ch.sem + 4 + q, src, ch.xr.at[q], ch.d1[q])
 
     def stage_d(ch):
         for q in (1, 2, 0):
-            recv(ch.sem + 4 + q, ch.xr.at[q], xdev[q])
-        for q, i in enumerate(around(zi) + [zi]):
+            recv(ch.sem + 4 + q, ch.xr.at[q], ch.d1[q])
+        for q, i in enumerate(around(ch.i2) + [ch.i2]):
             r = pl.multiple_of(i * ch.zb, ch.zb)
             rows = pl.ds(r, ch.zb)
-            v = ch.own[xi, rows]
+            v = ch.own[ch.i1, rows]
             for p in range(3):
                 v = v + (ch.xr[p, rows] if ch.k == 0 else decode(ch.xr.at[p], r, ch.zb))
             ch.zs[i] = v
-            if q < 3 and ch.k == 0:
-                send(ch.sem + 7 + q, ch.zs.at[i], ch.zr.at[q], zdev[q])
-            elif q < 3:
-                encode(ch.zs.at[i], ch.zx.at[q])
-                send(ch.sem + 7 + q, ch.zx.at[q], ch.zr.at[q], zdev[q])
+            if q < 3:
+                src = ch.zs.at[i]
+                if ch.k:
+                    encode(src, ch.zx.at[q])
+                    src = ch.zx.at[q]
+                send(ch.sem + 7 + q, src, ch.zr.at[q], ch.d2[q])
+
+    def source(i, q):
+        return lax.rem(i + 4 - hops[q], 4)
+
+    def pass_on(ch, p, i):
+        block = ch.g.at[core, ch.i1, i]
+        for q in range(3):
+            send(ch.sem + 13 + 3 * p + q, block, block, ch.d1[q])
 
     def stage_f(ch):
         for q in (1, 2, 0):
-            recv(ch.sem + 7 + q, ch.zr.at[q], zdev[q])
-        v = ch.zs[zi]
+            recv(ch.sem + 7 + q, ch.zr.at[q], ch.d2[q])
+        v = ch.zs[ch.i2]
         for p in range(3):
             v = v + (ch.zr[p] if ch.k == 0 else decode(ch.zr.at[p], 0, ch.zb))
-        ch.g[core, xi, zi] = v.astype(ch.g.dtype)
+        ch.g[core, ch.i1, ch.i2] = v.astype(ch.g.dtype)
         for q in range(3):
-            block = ch.g.at[core, xi, zi]
-            send(ch.sem + 10 + q, block, block, zdev[q])
-
-    def source(i, q):
-        return lax.rem(i + 4 - hops[q], 4)
+            block = ch.g.at[core, ch.i1, ch.i2]
+            send(ch.sem + 10 + q, block, block, ch.d2[q])
+        pass_on(ch, 0, ch.i2)
 
     def forward(ch, q, i):
-        send(ch.sem + 16 + q, ch.g.at[core, i], ch.g.at[core, i], partner)
+        send(ch.sem + 25 + q, ch.g.at[core, i], ch.g.at[core, i], partner)
+
+    def arrive(ch, q, p):
+        i = source(ch.i2, q)
+        recv(ch.sem + 10 + q, ch.g.at[core, ch.i1, i], ch.d2[q])
+        pass_on(ch, p, i)
+
+    def stage_g(ch):
+        arrive(ch, 1, 1)
+        arrive(ch, 2, 2)
 
     def stage_h(ch):
+        arrive(ch, 0, 3)
+        forward(ch, 3, ch.i1)
+
+    def stage_i(ch):
+        second = [ch.i2, source(ch.i2, 1), source(ch.i2, 2), source(ch.i2, 0)]
         for q in (1, 2, 0):
-            recv(ch.sem + 10 + q, ch.g.at[core, xi, source(zi, q)], zdev[q])
-        for q in range(3):
-            block = ch.g.at[core, xi]
-            send(ch.sem + 13 + q, block, block, xdev[q])
-        forward(ch, 3, xi)
-
-    def stage_i(ch):
-        for q in (1, 2, 0):
-            recv(ch.sem + 13 + q, ch.g.at[core, source(xi, q)], xdev[q])
-            forward(ch, q, source(xi, q))
+            i = source(ch.i1, q)
+            for p in range(4):
+                recv(ch.sem + 13 + 3 * p + q, ch.g.at[core, i, second[p]], ch.d1[q])
+            forward(ch, q, i)
 
     def stage_j(ch):
         for q in (3, 1, 2, 0):
-            i = xi if q == 3 else source(xi, q)
-            recv(ch.sem + 16 + q, ch.g.at[1 - core, i], partner)
+            i = ch.i1 if q == 3 else source(ch.i1, q)
+            recv(ch.sem + 25 + q, ch.g.at[1 - core, i], partner)
 
     begun = set()
 
@@ -292,14 +315,14 @@
         yx, yr = s["yx"][f], s["yr"][f]
         for q, i in enumerate(around(ctx)):
             encode(dp.at[i], yx.at[q])
-            send(ch.sem + 20 + q, yx.at[q], yr.at[q], ydev[q])
+            send(ch.sem + 29 + q, yx.at[q], yr.at[q], ydev[q])
 
     def stage_m(ch):
         if not ch.last:
             return
         f = ch.f
         for q in (1, 2, 0):
-            recv(ch.sem + 20 + q, s["yr"][f].at[q], ydev[q])
+            recv(ch.sem + 29 + q, s["yr"][f].at[q], ydev[q])
         n = outs[f].shape[0]
         yr = s["yr"][f]
         v = s["dp"][f][ctx]
@@ -314,13 +337,14 @@
                 dp[...] = jnp.zeros_like(dp)
         pl.semaphore_wait(barrier, len(peers))
 
-    stages = {"a": stage_a, "d": stage_d, "f": stage_f, "h": stage_h, "i": stage_i, "j": stage_j, "k": stage_k}
+    stages = {"s": stage_s, "a": stage_a, "d": stage_d, "f": stage_f, "g": stage_g, "h": stage_h,
+              "i": stage_i, "j": stage_j, "k": stage_k}
     for step in SCHEDULE:
         name, k = step[0], int(step[1:])
         if name == "p" and k == 0:
             stage_core()
         elif name == "p":
-            stage_probe(chunks[k], entry if k == 1 else None)
+            stage_probe(chunks[k])
         elif name == "t":
             stage_t(k)
         elif name == "w":
@@ -358,10 +382,10 @@
     xs = [x.T if turn else x for x, turn in zip(xs, turned)]
     fb = [-(-(f // 4) // 8) * 8 for f in fs]
     message_rows = [-(-n // 16) * 16 + SCALE_ROWS for n in fb]
-    pieces = [n for _, n in PLAN for _ in range(n)]
+    pieces = [n for _, n, _ in PLAN]
     count = SEMS * (1 + len(pieces))
     scratch = dict(
-        chunks=[chunk(r // 2, f32, True)] + [chunk(tokens // 2 // n, bf16, False) for n in pieces],
+        chunks=[chunk(r // 2, f32, True)] + [chunk(tokens * n // 16, bf16, False) for n in pieces],
         xv=[vm(x.shape, bf16) for x in xs], wv=[vm((f, r), bf16) for f in fs],
         bv=[vm((f, r), bf16) for f in fs], ev=[vm((1, r), f32) for f in fs],
         xt=[vm((8, 128) if turn else (f, tokens), bf16) for f, turn in zip(fs, turned)],
@@ -396,7 +420,7 @@
     return pl.pallas_call(
         body,
         out_shape=tuple(jax.ShapeDtypeStruct(v.shape, v.dtype) for v in values),
-        compiler_params=pltpu.CompilerParams(vmem_limit_bytes=2 * 2**20),
+        compiler_params=pltpu.CompilerParams(vmem_limit_bytes=60 * 2**20),
         name="place",
     )(*values)
 

time: 73.8 us -> 65.7 us (0.89)
  Pallas kernels: 70.3 us -> 64.7 us
  local copies, waits for them, and re-layouts: 2.61 us -> 0 us
    pallas_call x1, Pallas kernels: 69.6 us -> 63 us  [sketch(): pl.pallas_call(body, out_shape=[jax.ShapeDtypeStruct((f // 4, r), f32) fo...]
    unnamed x6 -> x0, local copies, waits for them, and re-layouts: 2.61 us -> none
    pallas_call x1, Pallas kernels: 0.76 us -> 1.75 us  [place(): pl.pallas_call(body, out_shape=tuple((jax.ShapeDtypeStruct(v.shape, v.dty...]
where the time goes in v3:
time: 65.7 us; the launch traced here: 65.4 us
  Pallas kernels  64.7 us (98%)
    pallas_call x1, Pallas kernels, sketch(): pl.pallas_call(body, out_shape=[jax.ShapeDtypeStruct((f // 4, r), f32) fo...  63 us
    pallas_call x1, Pallas kernels, place(): pl.pallas_call(body, out_shape=tuple((jax.ShapeDtypeStruct(v.shape, v.dty...  1.75 us

profile of v3, /device:TPU:1, one launch (start us, length us, event | category | flops | bytes accessed | tf_op | source)
XLA Modules:
  0.0 65.4 jit_solution(3795006898880605331)
XLA Ops:
  0.6 63.0 %sketch.1 = (f32[64,256]{1,0:T(8,128)}, f32[64,256]{1,0:T(8,128)}, f32[231,256]{1,0:T(8,128)}) custom-call(bf16[2048,256]{1,0:T(8,128)(2,1)} %refs_0_.1, bf16[2048,256]{1,0:T(8,128)(2,1)} %refs_1_.1, bf16[924,2048]{1,0:T(8,128)(2,1)} %bitcast.4, bf16[256,256]{1,0:T(8,128)(2,1)} %refs_3_.1, bf16[256,256]{1,0:T(8,128)(2,1)} %refs_4_.1, ...), custom_call_target="tpu_custom_call" | custom-call | tf_op jit(solution)/shard_map/sketch/pallas_call | solution.py:403
  63.6 1.8 %place.1 = (f32[64,256]{1,0:T(8,128)}, f32[64,256]{1,0:T(8,128)}, f32[231,256]{1,0:T(8,128)}) custom-call(f32[64,256]{1,0:T(8,128)} %get-tuple-element.6.refs_0_, f32[64,256]{1,0:T(8,128)} %get-tuple-element.7.refs_1_, f32[231,256]{1,0:T(8,128)} %get-tuple-element.8.refs_2_), custom_call_target="tpu_custom_call" | custom-call | tf_op jit(solution)/shard_map/place/pallas_call | solution.py:420

commit v4 on v3

--- a/solution.py
+++ b/solution.py
@@ -80,19 +80,24 @@
     xv, wv, bv, ev = s["xv"], s["wv"], s["bv"], s["ev"]
     factors = list(dict.fromkeys(f for f, _, _ in PLAN))
     loads = {}
+    begin, pieces = dict.fromkeys(factors, 0), []
+    for k, (f, n, _) in enumerate(PLAN):
+        for q, c in enumerate((1 - core, core)):
+            size = n * half // 8
+            rows = pl.ds(pl.multiple_of(c * half + begin[f], size), size)
+            where = (slice(None), rows) if turned[f] else rows
+            pieces.append(("x", f, q, begin[f]))
+            loads[pieces[-1]] = pltpu.make_async_copy(
+                xs[f].at[where], xv[f].at[where], lsem.at[9 + 2 * k + q])
+        begin[f] += n * half // 8
     for f in factors:
         loads["w", f] = pltpu.make_async_copy(ws[f], wv[f], lsem.at[f])
-        for q, c in enumerate((1 - core, core)):
-            rows = pl.ds(pl.multiple_of(c * half, half), half)
-            where = (slice(None), rows) if turned[f] else rows
-            loads["x", f, q] = pltpu.make_async_copy(
-                xs[f].at[where], xv[f].at[where], lsem.at[3 + 2 * f + q])
-        loads["b", f] = pltpu.make_async_copy(bs[f], bv[f], lsem.at[9 + f])
-        loads["e", f] = pltpu.make_async_copy(es[f], ev[f], lsem.at[12 + f])
+        loads["b", f] = pltpu.make_async_copy(bs[f], bv[f], lsem.at[3 + f])
+        loads["e", f] = pltpu.make_async_copy(es[f], ev[f], lsem.at[6 + f])
     first = factors[0]
-    order = [("w", first), ("x", first, 0), ("x", first, 1)]
+    order = [("w", first)] + pieces[:2]
     order += [("w", f) for f in factors[1:]] + [("b", f) for f in factors]
-    order += [("x", f, q) for f in factors[1:] for q in (0, 1)] + [("e", f) for f in factors]
+    order += pieces[2:] + [("e", f) for f in factors]
     for part in order:
         loads[part].start()
 
@@ -162,7 +167,7 @@
     def stage_probe(ch):
         load_wait("w", ch.f)
         for q, c, blocks in ((0, 1 - core, ch.cs), (1, core, ch.own)):
-            load_wait("x", ch.f, q)
+            load_wait("x", ch.f, q, ch.t0)
             for i in range(4):
                 tile_probe(ch.f, c * half + ch.t0 + i * ch.xb, blocks.at[i])
 
@@ -285,8 +290,9 @@
     def stage_t(f):
         if turned[f]:
             return
-        load_wait("x", f, 0)
-        load_wait("x", f, 1)
+        for piece in pieces:
+            if piece[1] == f:
+                load_wait(*piece)
         rows = xv[f].shape[1]
 
         @pl.loop(0, tokens // 256)
@@ -394,7 +400,7 @@
         yx=[vm((3, n, r), bf16) for n in message_rows],
         cfull=vm((r, r), f32), cpart=vm((2, 4, r // 8, r), f32), wp=vm((2, r, r), bf16),
         ssem=pltpu.SemaphoreType.DMA((count,)), rsem=pltpu.SemaphoreType.DMA((count,)),
-        lsem=pltpu.SemaphoreType.DMA((15,)),
+        lsem=pltpu.SemaphoreType.DMA((9 + 2 * len(PLAN),)),
     )
 
     def body(*refs):

time: 65.7 us -> 65.9 us (level)
  no operation moved by 1% of the time
where the time goes in v4:
time: 65.9 us; the launch traced here: 65.1 us
  Pallas kernels  64.5 us (98%)
    pallas_call x1, Pallas kernels, sketch(): pl.pallas_call(body, out_shape=[jax.ShapeDtypeStruct((f // 4, r), f32) fo...  62.7 us
    pallas_call x1, Pallas kernels, place(): pl.pallas_call(body, out_shape=tuple((jax.ShapeDtypeStruct(v.shape, v.dty...  1.75 us

profile of v4, /device:TPU:1, one launch (start us, length us, event | category | flops | bytes accessed | tf_op | source)
XLA Modules:
  0.0 65.1 jit_solution(5024443239291531193)
XLA Ops:
  0.6 62.7 %sketch.1 = (f32[64,256]{1,0:T(8,128)}, f32[64,256]{1,0:T(8,128)}, f32[231,256]{1,0:T(8,128)}) custom-call(bf16[2048,256]{1,0:T(8,128)(2,1)} %refs_0_.1, bf16[2048,256]{1,0:T(8,128)(2,1)} %refs_1_.1, bf16[924,2048]{1,0:T(8,128)(2,1)} %bitcast.4, bf16[256,256]{1,0:T(8,128)(2,1)} %refs_3_.1, bf16[256,256]{1,0:T(8,128)(2,1)} %refs_4_.1, ...), custom_call_target="tpu_custom_call" | custom-call | tf_op jit(solution)/shard_map/sketch/pallas_call | solution.py:409
  63.4 1.8 %place.1 = (f32[64,256]{1,0:T(8,128)}, f32[64,256]{1,0:T(8,128)}, f32[231,256]{1,0:T(8,128)}) custom-call(f32[64,256]{1,0:T(8,128)} %get-tuple-element.6.refs_0_, f32[64,256]{1,0:T(8,128)} %get-tuple-element.7.refs_1_, f32[231,256]{1,0:T(8,128)} %get-tuple-element.8.refs_2_), custom_call_target="tpu_custom_call" | custom-call | tf_op jit(solution)/shard_map/place/pallas_call | solution.py:426
